TPU v7x, 32 devices: a whole 2x2x4 slice. The times are simulated.
32 devices in a mesh: inputs: 8 (over z, y), tm: 4 (over x, core).
Axes of the slice: x: 2, y: 2, z: 4, core: 2. Of those that a mesh axis runs over, the one named last changes fastest.
Arguments:
- voltages: bfloat16 [128, 131072], P('inputs', 'tm'), may hold values from -8 to 8
- pfb_taps: float32 [8, 512], replicated, may hold values from -2 to 2
Outputs:
- visibilities: float32 [256, 1, 2, 128, 128], P(('inputs', 'tm'))
All inputs are finite; a program needn't handle non-finite values.
Results may differ from a plain program's by a relative error of at most 0.002.
Values may be sent and summed in bfloat16 or wider, within the bound.
No kernel may reach another device: no remote copies, remote signals or barrier semaphores. Data moves between devices by JAX's collectives and lax.ppermute only.
A program may use at most 128 MiB of HBM per device.

v0:
```python
import jax
import jax.numpy as jnp
from jax import lax
from jax.sharding import PartitionSpec as P

F = 256
TAPS = 8
TILE = 128
FRAME = 512


def from_behind(value, axis, steps):
    count = lax.axis_size(axis)
    initial, last = (max(0, -steps), min(count, count - steps))
    return lax.ppermute(value, axis, [(source, source + steps) for source in range(initial, last)])


def dft_table(chans, length):
    rows = jnp.arange(2 * chans, dtype=jnp.int32)
    freq = rows // 2
    part = rows % 2
    samp = jnp.arange(length, dtype=jnp.int32)
    phase = freq[:, None] * samp[None, :] % length
    angle = 2.0 * jnp.pi / length * phase.astype(jnp.float32)
    vals = jnp.where(part[:, None] == 0, jnp.cos(angle), -jnp.sin(angle))
    return (vals * (1.0 / length**0.5)).astype(jnp.bfloat16)


def tile_sums(spec, scale):
    left = jnp.concatenate([spec[:, 0], spec[:, 1]], axis=-1)
    twisted = jnp.concatenate([spec[:, 1], -spec[:, 0]], axis=-1)
    count_in = left.shape[1]
    blocks = count_in // TILE
    chans = left.shape[0]
    real_rows = []
    imag_rows = []
    for first in range(blocks):
        lower = first * TILE
        cols = left[:, lower:]
        real_part = jnp.einsum(
            "cik,cjk->cij", left[:, lower : lower + TILE], cols, preferred_element_type=jnp.float32
        )
        imag_part = jnp.einsum(
            "cik,cjk->cij",
            twisted[:, lower : lower + TILE],
            cols,
            preferred_element_type=jnp.float32,
        )
        count = blocks - first
        real_rows.append(real_part.reshape(chans, TILE, count, TILE).transpose(0, 2, 1, 3))
        imag_rows.append(imag_part.reshape(chans, TILE, count, TILE).transpose(0, 2, 1, 3))
    real_all = jnp.concatenate(real_rows, axis=1)
    imag_all = jnp.concatenate(imag_rows, axis=1)
    return jnp.stack([real_all, imag_all], axis=2) * scale


def on_device(voltages, pfb_taps):
    inp_local = voltages.shape[0]
    frames_local = voltages.shape[1] // FRAME
    previous = from_behind(voltages[:, voltages.shape[1] - (TAPS - 1) * FRAME :], "tm", 1)
    extended = jnp.concatenate([previous, voltages], axis=1).reshape(
        inp_local, frames_local + TAPS - 1, FRAME
    )
    filtered = jnp.zeros((inp_local, frames_local, FRAME), jnp.float32)
    for tap in range(TAPS):
        filtered = filtered + pfb_taps[tap][None, None, :] * extended[
            :, tap : tap + frames_local, :
        ].astype(jnp.float32)
    filtered = filtered.astype(jnp.bfloat16)
    table = dft_table(F, FRAME)
    spectra = jnp.einsum("kn,itn->kit", table, filtered, preferred_element_type=jnp.float32)
    spectra = spectra.astype(jnp.bfloat16).reshape(F, 2, inp_local, frames_local)
    blocks_time = lax.axis_size("tm")
    scale = 1.0 / (frames_local * blocks_time)
    turned = lax.all_to_all(
        lax.all_to_all(spectra, "inputs", split_axis=0, concat_axis=2, tiled=True),
        "tm",
        split_axis=0,
        concat_axis=3,
        tiled=True,
    )
    return tile_sums(turned, scale)


def solution(mesh):
    in_specs = (P("inputs", "tm"), P())
    out_specs = P(("inputs", "tm"), None, None, None, None)
    return jax.shard_map(
        on_device, mesh=mesh, in_specs=in_specs, out_specs=out_specs, check_vma=False
    )
```

profile of v0, /device:TPU:0, one launch (start us, length us, event | category | flops | bytes accessed | tf_op | source)
XLA Modules:
  0.0 76.3 jit_solution(17021184768935166234)
XLA Ops:
  0.0 0.9 %slice.60 = bf16[16,3584]{1,0:T(8,128)(2,1)S(1)} slice(bf16[16,32768]{1,0:T(8,128)(2,1)} %param.2), slice={[0:16], [29184:32768]} | slice | bytes 229376 | tf_op jit(solution)/shard_map/slice | solution.py:60
  0.9 2.4 %collective-permute-start = (bf16[16,3584]{1,0:T(8,128)(2,1)S(1)}, bf16[16,3584]{1,0:T(8,128)(2,1)S(1)}, u32[]{:S(2)}, u32[]{:S(2)}) collective-permute-start(bf16[16,3584]{1,0:T(8,128)(2,1)S(1)} %slice.60), channel_id=1, source_target_pairs={{0,1},{1,2},{2,3},{4,5},{5,6},{6,7},{8,9},{9,10},{10,11},{12,13},{... | collective-permute-start | bytes 344072 | tf_op jit(solution)/shard_map/ppermute | solution.py:15
  3.3 1.0 %fusion.32 = (f32[1,512]{1,0:T(1,128)S(1)}, f32[1,512]{1,0:T(1,128)S(1)}, f32[1,512]{1,0:T(1,128)S(1)}, f32[1,512]{1,0:T(1,128)S(1)}, f32[1,512]{1,0:T(1,128)S(1...) fusion(f32[8,512]{1,0:T(8,128)} %param.3), kind=kLoop, calls=%fused_computation.48 | loop fusion | bytes 32768 | tf_op jit(solution)/shard_map/slice | solution.py:66
  4.4 0.0 collective-permute-done
  4.4 1.3 %pad_maximum_fusion = bf16[16,36352]{1,0:T(8,128)(2,1)S(1)} fusion(bf16[16,32768]{1,0:T(8,128)(2,1)} %param.2, bf16[16,3584]{1,0:T(8,128)(2,1)S(1)} %collective-permute-done), kind=kLoop, calls=%fused_computation.7 | loop fusion | flops 2326528 | bytes 2326528 | tf_op jit(solution)/shard_map/concatenate | solution.py:61
  5.7 0.7 reshape.74
  6.4 6.5 %convolution_convert_fusion = bf16[512,16,64]{0,2,1:T(8,128)(2,1)S(1)} fusion(bf16[16,71,512]{2,1,0:T(8,128)(2,1)S(1)} %reshape.74, f32[512]{0:T(512)S(1)} %bitcast.42, f32[512]{0:T(512)S(1)} %bitcast.43, f32[512]{0:T(512)S(1)} %bitcast.37, f32[512]{0:T(512)S(1)} %bitcast.38, f32[512]{0:T(512)S(1)} %bitcast.39, f32[512]{0:T(512)S(1)} %bitcast.40, ...), kind=kOutput, calls=%fused_computation.4 | convolution fusion | flops 554696704 | bytes 9456128 | tf_op jit(solution)/shard_map/kn,itn->kit/dot_general | solution.py:71
  12.9 2.0 %copy.11 = bf16[512,16,64]{2,1,0:T(8,128)(2,1)S(1)} copy(bf16[512,16,64]{0,2,1:T(8,128)(2,1)S(1)} %convolution_convert_fusion) | data formatting | bytes 2097152 | tf_op jit(solution)/shard_map/convert_element_type | solution.py:72
  15.0 1.7 %reshape.77 = bf16[8,2,32768]{2,1,0:T(2,128)(2,1)S(1)} reshape(bf16[256,2,16,64]{3,2,1,0:T(8,128)(2,1)S(1)} %bitcast.27) | data formatting | bytes 2097152
  16.7 32.5 %all_to_all.36 = bf16[8,2,32768]{2,1,0:T(2,128)(2,1)} all-to-all(bf16[8,2,32768]{2,1,0:T(2,128)(2,1)S(1)} %reshape.77), channel_id=1, replica_groups=mesh['inputs'=8,'tm'=4] {'inputs'}, dimensions={0} | all-to-all | bytes 2097152 | tf_op jit(solution)/shard_map/all_to_all | solution.py:76
  49.1 3.1 %reshape.78 = bf16[256,2,16,64]{3,2,1,0:T(8,128)(2,1)S(1)} reshape(bf16[8,2,32768]{2,1,0:T(2,128)(2,1)} %all_to_all.36) | data formatting | bytes 2097152
  52.2 2.0 %copy.12 = bf16[8,32,2,16,64]{4,3,0,2,1:T(8,128)(2,1)} copy(bf16[8,32,2,16,64]{4,3,2,1,0:T(8,128)(2,1)S(1)} %bitcast.28) | data formatting | bytes 2097152 | tf_op jit(solution)/shard_map/all_to_all | solution.py:76
  54.2 2.0 %copy.13 = bf16[32,2,128,64]{2,3,1,0:T(8,128)(2,1)S(1)} copy(bf16[32,2,128,64]{3,2,1,0:T(8,128)(2,1)} %bitcast.29) | data formatting | bytes 2097152 | tf_op jit(solution)/shard_map/all_to_all | solution.py:76
  56.2 17.4 %all_to_all.37 = bf16[32,2,128,64]{2,3,1,0:T(8,128)(2,1)S(1)} all-to-all(bf16[32,2,128,64]{2,3,1,0:T(8,128)(2,1)S(1)} %copy.13), channel_id=1, replica_groups=mesh['inputs'=8,'tm'=4] {'tm'}, dimensions={0} | all-to-all | bytes 2097152 | tf_op jit(solution)/shard_map/all_to_all | solution.py:75
  73.6 0.1 copy.14
  73.7 0.1 fusion.31
  73.8 0.2 copy.19
  74.0 0.2 copy.18
  74.3 0.4 convolution_bitcast_fusion.1
  74.7 0.4 convolution_bitcast_fusion
  75.2 0.1 maximum_multiply_fusion
  75.3 1.1 %copy.17 = f32[8,1,2,128,128]{4,3,2,1,0:T(8,128)} copy(f32[8,1,2,128,128]{4,3,0,2,1:T(8,128)S(1)} %maximum_multiply_fusion) | data formatting | bytes 2097152 | tf_op jit(solution)/shard_map/mul | solution.py:54
  (3 shorter events, 0.0 us)
Async XLA Ops:
  0.9 3.5 %collective-permute-start = (bf16[16,3584]{1,0:T(8,128)(2,1)S(1)}, bf16[16,3584]{1,0:T(8,128)(2,1)S(1)}, u32[]{:S(2)}, u32[]{:S(2)}) collective-permute-start(bf16[16,3584]{1,0:T(8,128)(2,1)S(1)} %slice.60), channel_id=1, source_target_pairs={{0,1},{1,2},{2,3},{4,5},{5,6},{6,7},{8,9},{9,10},{10,11},{12,13},{... | collective-permute-start | bytes 344072 | tf_op jit(solution)/shard_map/ppermute | solution.py:15
where the time goes:
time: 76.7 us; the launch traced here: 76.3 us
  blocking collectives  49.9 us (65%)
  local copies, waits for them, and re-layouts  15.1 us (20%)
  matrix products  7.4 us (10%)
  starting transfers between devices  2.39 us (3%)
  other arithmetic  1.43 us (2%)
    all_to_all x1, blocking collectives, on_device(): lax.all_to_all(spectra, 'inputs', split_axis=0, concat_axis=2, tiled=True)  32.5 us
    all_to_all x1, blocking collectives, on_device(): lax.all_to_all(lax.all_to_all(spectra, 'inputs', split_axis=0, concat_axi...  17.4 us
    dot_general x1, matrix products, on_device(): jnp.einsum('kn,itn->kit', table, filtered, preferred_element_type=jnp.flo...  6.55 us
    unnamed x4, local copies, waits for them, and re-layouts  5.2 us
    all_to_all x2, local copies, waits for them, and re-layouts, on_device(): lax.all_to_all(spectra, 'inputs', split_axis=0, concat_axis=2, tiled=True)  3.96 us
    ppermute x1, starting transfers between devices, from_behind(): lax.ppermute(value, axis, [(source, source + steps) for source in range(i...  2.39 us
    convert_element_type x1, local copies, waits for them, and re-layouts, on_device(): spectra.astype(jnp.bfloat16).reshape(F, 2, inp_local, frames_local)  2.03 us
  transfers between devices with their start and end apart: 1, of which 0 were waited for; matrix products, arithmetic and copies ran while one was open for 1% of the time, Pallas kernels for 0%

commit v1 on v0

--- a/solution.py
+++ b/solution.py
@@ -7,6 +7,28 @@
 TAPS = 8
 TILE = 128
 FRAME = 512
+
+
+def in_blocks(array, dim, size):
+    before, after = (array.shape[:dim], array.shape[dim + 1 :])
+    return jnp.moveaxis(array.reshape(*before, size, -1, *after), dim, 0)
+
+
+def laid_out(parts, dim):
+    shape = list(parts.shape[1:])
+    shape[dim] *= parts.shape[0]
+    return jnp.moveaxis(parts, 0, dim).reshape(shape)
+
+
+def exchange_in_pairs(shard, axis, split_dim, concat_dim):
+    size, index = (lax.axis_size(axis), lax.axis_index(axis))
+    blocks = in_blocks(shard, split_dim, size)
+    gathered = [blocks[index]]
+    for lap in range(1, size):
+        sent = blocks[index ^ lap]
+        gathered.append(lax.ppermute(sent, axis, [(i, i ^ lap) for i in range(size)]))
+    blocks = jnp.stack(gathered)[index ^ jnp.arange(size)]
+    return laid_out(blocks, concat_dim)
 
 
 def from_behind(value, axis, steps):
@@ -72,12 +94,8 @@
     spectra = spectra.astype(jnp.bfloat16).reshape(F, 2, inp_local, frames_local)
     blocks_time = lax.axis_size("tm")
     scale = 1.0 / (frames_local * blocks_time)
-    turned = lax.all_to_all(
-        lax.all_to_all(spectra, "inputs", split_axis=0, concat_axis=2, tiled=True),
-        "tm",
-        split_axis=0,
-        concat_axis=3,
-        tiled=True,
+    turned = exchange_in_pairs(
+        lax.all_to_all(spectra, "inputs", split_axis=0, concat_axis=2, tiled=True), "tm", 0, 3
     )
     return tile_sums(turned, scale)
 

time: 76.7 us -> 71.6 us (0.934)
  blocking collectives: 49.9 us -> 0 us
  waiting for transfers between devices: 0.01 us -> 37.5 us
  starting transfers between devices: 2.39 us -> 11.5 us
  local copies, waits for them, and re-layouts: 15.1 us -> 12.8 us
    all_to_all x2 -> x0, blocking collectives: 49.9 us -> none  [the longest x1 32.5 us: on_device(): lax.all_to_all(spectra, 'inputs', split_axis=0, concat_axis=2, tiled=True)]
    all_to_all x0 -> x1, waiting for transfers between devices: none -> 26.5 us  [on_device(): lax.all_to_all(spectra, 'inputs', split_axis=0, concat_axis=2, tiled=True)]
    ppermute x0 -> x3, waiting for transfers between devices: none -> 11 us  [exchange_in_pairs(): lax.ppermute(sent, axis, [(i, i ^ lap) for i in range(size)])]
    all_to_all x0 -> x1, starting transfers between devices: none -> 6.65 us  [on_device(): lax.all_to_all(spectra, 'inputs', split_axis=0, concat_axis=2, tiled=True)]
    all_to_all x2 -> x1, local copies, waits for them, and re-layouts: 3.96 us -> 0.61 us  [on_device(): lax.all_to_all(spectra, 'inputs', split_axis=0, concat_axis=2, tiled=True)]
    ppermute x0 -> x3, starting transfers between devices: none -> 2.47 us  [exchange_in_pairs(): lax.ppermute(sent, axis, [(i, i ^ lap) for i in range(size)])]
    dynamic_slice x0 -> x4, local copies, waits for them, and re-layouts: none -> 0.8 us  [the longest x3 0.66 us: exchange_in_pairs(): sent = blocks[index ^ lap]]
    unnamed x4 -> x5, local copies, waits for them, and re-layouts: 5.2 us -> 4.73 us
  transfers between devices with their start and end apart: 1 -> 5, of which waited for: 0 -> 3; matrix products, arithmetic and copies ran while one was open for 1% -> 2% of each run, Pallas kernels for 0% -> 0%
where the time goes in v1:
time: 71.6 us; the launch traced here: 71 us
  waiting for transfers between devices  37.5 us (52%)
  local copies, waits for them, and re-layouts  12.8 us (18%)
  starting transfers between devices  11.5 us (16%)
  matrix products  7.41 us (10%)
  other arithmetic  1.58 us (2%)
    all_to_all x1, waiting for transfers between devices, on_device(): lax.all_to_all(spectra, 'inputs', split_axis=0, concat_axis=2, tiled=True)  26.5 us
    ppermute x3, waiting for transfers between devices, exchange_in_pairs(): lax.ppermute(sent, axis, [(i, i ^ lap) for i in range(size)])  11 us
    all_to_all x1, starting transfers between devices, on_device(): lax.all_to_all(spectra, 'inputs', split_axis=0, concat_axis=2, tiled=True)  6.65 us
    dot_general x1, matrix products, on_device(): jnp.einsum('kn,itn->kit', table, filtered, preferred_element_type=jnp.flo...  6.55 us
    unnamed x5, local copies, waits for them, and re-layouts  4.73 us
    ppermute x3, starting transfers between devices, exchange_in_pairs(): lax.ppermute(sent, axis, [(i, i ^ lap) for i in range(size)])  2.47 us
    ppermute x1, starting transfers between devices, from_behind(): lax.ppermute(value, axis, [(source, source + steps) for source in range(i...  2.39 us
    convert_element_type x1, local copies, waits for them, and re-layouts, on_device(): spectra.astype(jnp.bfloat16).reshape(F, 2, inp_local, frames_local)  2.03 us
  transfers between devices with their start and end apart: 5, of which 3 were waited for; matrix products, arithmetic and copies ran while one was open for 2% of the time, Pallas kernels for 0%

profile of v1, /device:TPU:0, one launch (start us, length us, event | category | flops | bytes accessed | tf_op | source)
XLA Modules:
  0.0 71.0 jit_solution(3748333076297289736)
XLA Ops:
  0.0 0.9 %slice.60 = bf16[16,3584]{1,0:T(8,128)(2,1)S(1)} slice(bf16[16,32768]{1,0:T(8,128)(2,1)} %param.2), slice={[0:16], [29184:32768]} | slice | bytes 229376 | tf_op jit(solution)/shard_map/slice | solution.py:82
  0.9 2.4 %collective-permute-start = (bf16[16,3584]{1,0:T(8,128)(2,1)S(1)}, bf16[16,3584]{1,0:T(8,128)(2,1)S(1)}, u32[]{:S(2)}, u32[]{:S(2)}) collective-permute-start(bf16[16,3584]{1,0:T(8,128)(2,1)S(1)} %slice.60), channel_id=1, source_target_pairs={{0,1},{1,2},{2,3},{4,5},{5,6},{6,7},{8,9},{9,10},{10,11},{12,13},{... | collective-permute-start | bytes 344072 | tf_op jit(solution)/shard_map/ppermute | solution.py:37
  3.3 1.0 %fusion.33 = (f32[1,512]{1,0:T(1,128)S(1)}, f32[1,512]{1,0:T(1,128)S(1)}, f32[1,512]{1,0:T(1,128)S(1)}, f32[1,512]{1,0:T(1,128)S(1)}, f32[1,512]{1,0:T(1,128)S(1...) fusion(f32[8,512]{1,0:T(8,128)} %param.3), kind=kLoop, calls=%fused_computation.57 | loop fusion | bytes 32768 | tf_op jit(solution)/shard_map/slice | solution.py:88
  4.4 0.0 collective-permute-done
  4.4 1.3 %pad_maximum_fusion = bf16[16,36352]{1,0:T(8,128)(2,1)S(1)} fusion(bf16[16,32768]{1,0:T(8,128)(2,1)} %param.2, bf16[16,3584]{1,0:T(8,128)(2,1)S(1)} %collective-permute-done), kind=kLoop, calls=%fused_computation.8 | loop fusion | flops 2326528 | bytes 2326528 | tf_op jit(solution)/shard_map/concatenate | solution.py:83
  5.7 0.7 reshape.97
  6.4 6.5 %convolution_convert_fusion = bf16[512,16,64]{0,2,1:T(8,128)(2,1)S(1)} fusion(bf16[16,71,512]{2,1,0:T(8,128)(2,1)S(1)} %reshape.97, f32[512]{0:T(512)S(1)} %bitcast.54, f32[512]{0:T(512)S(1)} %bitcast.55, f32[512]{0:T(512)S(1)} %bitcast.49, f32[512]{0:T(512)S(1)} %bitcast.50, f32[512]{0:T(512)S(1)} %bitcast.51, f32[512]{0:T(512)S(1)} %bitcast.52, ...), kind=kOutput, calls=%fused_computation.5 | convolution fusion | flops 554696704 | bytes 9456128 | tf_op jit(solution)/shard_map/kn,itn->kit/dot_general | solution.py:93
  12.9 2.0 %copy.4 = bf16[512,16,64]{2,1,0:T(8,128)(2,1)S(1)} copy(bf16[512,16,64]{0,2,1:T(8,128)(2,1)S(1)} %convolution_convert_fusion) | data formatting | bytes 2097152 | tf_op jit(solution)/shard_map/convert_element_type | solution.py:94
  15.0 2.7 %reshape.110 = bf16[8,2,32768]{2,1,0:T(2,128)(2,1)} reshape(bf16[256,2,16,64]{3,2,1,0:T(8,128)(2,1)S(1)} %bitcast.34) | data formatting | bytes 2097152
  17.6 6.7 %all-to-all-start = ((bf16[8,2,32768]{2,1,0:T(2,128)(2,1)}), bf16[8,2,32768]{2,1,0:T(2,128)(2,1)S(1)}, u32[]{:S(2)}, u32[]{:S(2)}) async-start(bf16[8,2,32768]{2,1,0:T(2,128)(2,1)} %reshape.110), calls=%async_computation | async-start | bytes 2097152 | tf_op jit(solution)/shard_map/all_to_all | solution.py:98
  24.3 26.5 %all-to-all-done = bf16[8,2,32768]{2,1,0:T(2,128)(2,1)S(1)} async-done(((bf16[8,2,32768]{2,1,0:T(2,128)(2,1)}), bf16[8,2,32768]{2,1,0:T(2,128)(2,1)S(1)}, u32[]{:S(2)}, u32[]{:S(2)}) %all-to-all-start) | async-done | bytes 1048608 | tf_op jit(solution)/shard_map/all_to_all | solution.py:98
  50.8 1.4 %reshape.111 = bf16[256,2,16,64]{3,2,1,0:T(8,128)(2,1)S(1)} reshape(bf16[8,2,32768]{2,1,0:T(2,128)(2,1)S(1)} %all-to-all-done) | data formatting | bytes 2097152
  52.2 0.6 copy.5
  52.8 0.1 constant_dynamic-slice_fusion.3
  53.0 0.2 copy.7
  53.2 1.0 %collective-permute-start.1 = (bf16[8,2,128,64]{2,3,1,0:T(8,128)(2,1)S(1)}, bf16[8,2,128,64]{2,3,1,0:T(8,128)(2,1)S(1)}, u32[]{:S(2)}, u32[]{:S(2)}) collective-permute-start(bf16[8,2,128,64]{2,3,1,0:T(8,128)(2,1)S(1)} %bitcast.42), channel_id=1, source_target_pairs={{0,1},{1,0},{2,3},{3,2},{4,5},{5,4},{6,7},{7,6},{8,9},{9,8},{10,11... | collective-permute-start | bytes 786440 | tf_op jit(solution)/shard_map/ppermute | solution.py:29
  54.2 0.2 copy.8
  54.4 0.7 %collective-permute-start.2 = (bf16[8,2,128,64]{2,3,1,0:T(8,128)(2,1)S(1)}, bf16[8,2,128,64]{2,3,1,0:T(8,128)(2,1)S(1)}, u32[]{:S(2)}, u32[]{:S(2)}) collective-permute-start(bf16[8,2,128,64]{2,3,1,0:T(8,128)(2,1)S(1)} %bitcast.43), channel_id=1, source_target_pairs={{0,2},{1,3},{2,0},{3,1},{4,6},{5,7},{6,4},{7,5},{8,10},{9,11},{10,... | collective-permute-start | bytes 786440 | tf_op jit(solution)/shard_map/ppermute | solution.py:29
  55.1 0.2 copy.9
  55.4 0.8 %collective-permute-start.3 = (bf16[8,2,128,64]{2,3,1,0:T(8,128)(2,1)S(1)}, bf16[8,2,128,64]{2,3,1,0:T(8,128)(2,1)S(1)}, u32[]{:S(2)}, u32[]{:S(2)}) collective-permute-start(bf16[8,2,128,64]{2,3,1,0:T(8,128)(2,1)S(1)} %bitcast.44), channel_id=1, source_target_pairs={{0,3},{1,2},{2,1},{3,0},{4,7},{5,6},{6,5},{7,4},{8,11},{9,10},{10,... | collective-permute-start | bytes 786440 | tf_op jit(solution)/shard_map/ppermute | solution.py:29
  56.1 0.2 copy.14
  56.4 0.0 collective-permute-done.1
  56.4 7.3 %collective-permute-done.2 = bf16[8,2,128,64]{2,3,1,0:T(8,128)(2,1)S(1)} collective-permute-done((bf16[8,2,128,64]{2,3,1,0:T(8,128)(2,1)S(1)}, bf16[8,2,128,64]{2,3,1,0:T(8,128)(2,1)S(1)}, u32[]{:S(2)}, u32[]{:S(2)}) %collective-permute-start.2) | collective-permute-done | bytes 262176 | tf_op jit(solution)/shard_map/ppermute | solution.py:29
  63.7 3.7 %collective-permute-done.3 = bf16[8,2,128,64]{2,3,1,0:T(8,128)(2,1)S(1)} collective-permute-done((bf16[8,2,128,64]{2,3,1,0:T(8,128)(2,1)S(1)}, bf16[8,2,128,64]{2,3,1,0:T(8,128)(2,1)S(1)}, u32[]{:S(2)}, u32[]{:S(2)}) %collective-permute-start.3) | collective-permute-done | bytes 262176 | tf_op jit(solution)/shard_map/ppermute | solution.py:29
  67.4 0.1 pad_maximum_fusion.1
  67.5 0.7 %gather_fusion = bf16[4,8,2,128,64]{3,4,2,1,0:T(8,128)(2,1)S(1)} fusion(bf16[4,8,2,128,64]{3,4,2,1,0:T(8,128)(2,1)S(1)} %pad_maximum_fusion.1, s32[1024]{0:T(1024)S(1)} %pad_clamp_fusion), kind=kCustom, calls=%fused_computation | custom fusion | bytes 2097168 | tf_op jit(solution)/shard_map/gather | solution.py:30
  68.2 0.1 copy.10
  68.3 0.1 fusion.32
  68.4 0.2 copy.15
  68.7 0.2 copy.16
  68.9 0.4 convolution_bitcast_fusion.1
  69.4 0.4 convolution_bitcast_fusion
  69.8 0.1 maximum_multiply_fusion
  69.9 1.1 %copy.13 = f32[8,1,2,128,128]{4,3,2,1,0:T(8,128)} copy(f32[8,1,2,128,128]{4,3,0,2,1:T(8,128)S(1)} %maximum_multiply_fusion) | data formatting | bytes 2097152 | tf_op jit(solution)/shard_map/mul | solution.py:76
  (5 shorter events, 0.1 us)
Async XLA Ops:
  0.9 3.5 %collective-permute-start = (bf16[16,3584]{1,0:T(8,128)(2,1)S(1)}, bf16[16,3584]{1,0:T(8,128)(2,1)S(1)}, u32[]{:S(2)}, u32[]{:S(2)}) collective-permute-start(bf16[16,3584]{1,0:T(8,128)(2,1)S(1)} %slice.60), channel_id=1, source_target_pairs={{0,1},{1,2},{2,3},{4,5},{5,6},{6,7},{8,9},{9,10},{10,11},{12,13},{... | collective-permute-start | bytes 344072 | tf_op jit(solution)/shard_map/ppermute | solution.py:37
  17.6 33.1 %all-to-all-start = ((bf16[8,2,32768]{2,1,0:T(2,128)(2,1)}), bf16[8,2,32768]{2,1,0:T(2,128)(2,1)S(1)}, u32[]{:S(2)}, u32[]{:S(2)}) async-start(bf16[8,2,32768]{2,1,0:T(2,128)(2,1)} %reshape.110), calls=%async_computation | async-start | bytes 2097152 | tf_op jit(solution)/shard_map/all_to_all | solution.py:98
  53.2 3.2 %collective-permute-start.1 = (bf16[8,2,128,64]{2,3,1,0:T(8,128)(2,1)S(1)}, bf16[8,2,128,64]{2,3,1,0:T(8,128)(2,1)S(1)}, u32[]{:S(2)}, u32[]{:S(2)}) collective-permute-start(bf16[8,2,128,64]{2,3,1,0:T(8,128)(2,1)S(1)} %bitcast.42), channel_id=1, source_target_pairs={{0,1},{1,0},{2,3},{3,2},{4,5},{5,4},{6,7},{7,6},{8,9},{9,8},{10,11... | collective-permute-start | bytes 786440 | tf_op jit(solution)/shard_map/ppermute | solution.py:29
  54.4 9.2 %collective-permute-start.2 = (bf16[8,2,128,64]{2,3,1,0:T(8,128)(2,1)S(1)}, bf16[8,2,128,64]{2,3,1,0:T(8,128)(2,1)S(1)}, u32[]{:S(2)}, u32[]{:S(2)}) collective-permute-start(bf16[8,2,128,64]{2,3,1,0:T(8,128)(2,1)S(1)} %bitcast.43), channel_id=1, source_target_pairs={{0,2},{1,3},{2,0},{3,1},{4,6},{5,7},{6,4},{7,5},{8,10},{9,11},{10,... | collective-permute-start | bytes 786440 | tf_op jit(solution)/shard_map/ppermute | solution.py:29
  55.4 12.0 %collective-permute-start.3 = (bf16[8,2,128,64]{2,3,1,0:T(8,128)(2,1)S(1)}, bf16[8,2,128,64]{2,3,1,0:T(8,128)(2,1)S(1)}, u32[]{:S(2)}, u32[]{:S(2)}) collective-permute-start(bf16[8,2,128,64]{2,3,1,0:T(8,128)(2,1)S(1)} %bitcast.44), channel_id=1, source_target_pairs={{0,3},{1,2},{2,1},{3,0},{4,7},{5,6},{6,5},{7,4},{8,11},{9,10},{10,... | collective-permute-start | bytes 786440 | tf_op jit(solution)/shard_map/ppermute | solution.py:29
